TPU v7x, 32 devices: a whole 2x2x4 slice. The times are simulated.
32 devices in a mesh: dap: 8 (over y, x, core), dp: 4 (over z).
Axes of the slice: x: 2, y: 2, z: 4, core: 2. Of those that a mesh axis runs over, the one named last changes fastest.
Arguments:
- pair: bfloat16 [64, 16, 128], P(('dp', 'dap')), parts along dimension 0, may hold values from -6 to 6
- pair_mask: int32 [64, 16], P(('dp', 'dap')), parts along dimension 0, may hold values from 0 to 1, as said below
- w_left: bfloat16 [128, 256], replicated, may hold values from -0.5 to 0.5
- w_right: bfloat16 [128, 256], replicated, may hold values from -0.5 to 0.5
- w_tri_gate: bfloat16 [128, 128], replicated, may hold values from -0.5 to 0.5
- w_tri_out: bfloat16 [128, 128], replicated, may hold values from -0.5 to 0.5
- w_attend: bfloat16 [128, 512], replicated, may hold values from -0.5 to 0.5
- w_bias: bfloat16 [128, 4], replicated
- w_att_out: bfloat16 [128, 128], replicated, may hold values from -0.5 to 0.5
Outputs:
- pair_out: float32 [64, 16, 128], P('dp', 'dap'), parts along dimension 0
There are 4 independent parts, one for each index of `dp`. A program takes and returns all parts, laid end to end along the dimension named above; an argument that names none is the same for every part. Nothing has to cross between parts.
Inputs may be any that keep to these rules, and one draw needn't show every extreme that they name: pair_mask[i, i] = 1 for every residue i.
All inputs are finite; a program needn't handle non-finite values.
Results may differ from a plain program's by a relative error of at most 0.014.
The roundings to bfloat16 on the way count: a program that leaves them out, or rounds other values in their place, can miss the bound.
Values may be sent and summed in bfloat16 or wider, within the bound.
No kernel may reach another device: no remote copies, remote signals or barrier semaphores. Data moves between devices by JAX's collectives and lax.ppermute only.
A program may use at most 128 MiB of HBM per device.

v0:
```python
import jax
import jax.numpy as jnp
from jax import lax
from jax.sharding import PartitionSpec as P


def layer_norm(x):
    x = x.astype(jnp.float32)
    mean = jnp.mean(x, axis=-1, keepdims=True)
    var = jnp.mean((x - mean) * (x - mean), axis=-1, keepdims=True)
    return (x - mean) / jnp.sqrt(var + 1e-05)


def matmul(x, w):
    flat = x.reshape(-1, x.shape[-1])
    return jnp.dot(flat, w, preferred_element_type=jnp.float32).reshape(
        x.shape[:-1] + (w.shape[1],)
    )


def edges(zn, weight, maskf, hidden):
    both = matmul(zn, weight)
    return (jax.nn.sigmoid(both[..., :hidden]) * both[..., hidden:] * maskf[..., None]).astype(
        jnp.bfloat16
    )


def triangle_update(pair_part, zn_part, tri, w_tri_gate, w_tri_out):
    tn = layer_norm(tri).astype(jnp.bfloat16)
    update = jax.nn.sigmoid(matmul(zn_part, w_tri_gate)) * matmul(tn, w_tri_out)
    return pair_part.astype(jnp.float32) + update


def attention(pair1, mask_cols, w_attend, w_bias, w_att_out):
    inner = w_att_out.shape[0]
    heads = w_bias.shape[1]
    head_dim = inner // heads
    total, local = (pair1.shape[0], pair1.shape[1])
    yn = layer_norm(pair1).astype(jnp.bfloat16)
    proj = matmul(yn, w_attend)
    query = proj[..., :inner].astype(jnp.bfloat16).reshape(total, local, heads, head_dim)
    keys = proj[..., inner : 2 * inner].astype(jnp.bfloat16).reshape(total, local, heads, head_dim)
    values = (
        proj[..., 2 * inner : 3 * inner].astype(jnp.bfloat16).reshape(total, local, heads, head_dim)
    )
    gate = jax.nn.sigmoid(proj[..., 3 * inner :])
    bias_part = jnp.einsum("kic,ch->hki", yn, w_bias, preferred_element_type=jnp.float32).astype(
        jnp.bfloat16
    )
    bias = lax.all_gather(bias_part, "dap", axis=2, tiled=True)
    scores = jnp.einsum(
        "irhd,krhd->rhki", query, keys, preferred_element_type=jnp.float32
    ) / jnp.sqrt(jnp.float32(head_dim))
    scores = scores + bias.astype(jnp.float32)[None]
    live = jnp.transpose(mask_cols.astype(jnp.float32))[:, None, :, None]
    scores = jnp.where(live > 0.5, scores, jnp.float32(-1000000000.0))
    weights = jax.nn.softmax(scores, axis=2).astype(jnp.bfloat16)
    summed = jnp.einsum(
        "rhki,krhd->irhd", weights, values, preferred_element_type=jnp.float32
    ).reshape(total, local, inner)
    att = (gate * summed).astype(jnp.bfloat16)
    return pair1 + matmul(att, w_att_out)


def shards(pair, pair_mask, w_left, w_right, w_tri_gate, w_tri_out, w_attend, w_bias, w_att_out):
    hidden = w_tri_out.shape[0]
    maskf = pair_mask.astype(jnp.float32)
    zn = layer_norm(pair).astype(jnp.bfloat16)
    left_edge = edges(zn, w_left, maskf, hidden)
    right_edge = edges(zn, w_right, maskf, hidden)
    pair_cols, mask_cols = (
        lax.all_to_all(pair, "dap", split_axis=1, concat_axis=0, tiled=True),
        lax.all_to_all(
            pair_mask.astype(jnp.bfloat16), "dap", split_axis=1, concat_axis=0, tiled=True
        ),
    )
    tri = jnp.einsum(
        "ikc,jkc->ijc",
        lax.all_gather(left_edge, "dap", axis=0, tiled=True),
        right_edge,
        preferred_element_type=jnp.float32,
    )
    zn_cols = layer_norm(pair_cols).astype(jnp.bfloat16)
    pair1 = triangle_update(pair_cols, zn_cols, tri, w_tri_gate, w_tri_out)
    return attention(pair1, mask_cols, w_attend, w_bias, w_att_out)


def solution(mesh):
    placed = (
        P(("dp", "dap"), None, None),
        P(("dp", "dap"), None),
        P(),
        P(),
        P(),
        P(),
        P(),
        P(),
        P(),
    )
    return jax.shard_map(
        shards, mesh=mesh, in_specs=placed, out_specs=P("dp", "dap", None), check_vma=False
    )
```

profile of v0, /device:TPU:0, one launch (start us, length us, event | category | flops | bytes accessed | tf_op | source)
XLA Modules:
  0.0 41.4 jit_solution(9851496634011292177)
XLA Ops:
  0.0 0.8 %fusion.56 = (bf16[2,16]{1,0:T(2,128)(2,1)S(1)}, f32[2,16]{1,0:T(2,128)S(1)}) fusion(s32[2,16]{1,0:T(2,128)} %param.10), kind=kLoop, calls=%fused_computation.85 | loop fusion | flops 64 | bytes 320 | tf_op jit(solution)/shard_map/convert_element_type | solution.py:74
  0.8 0.6 %copy.53 = bf16[2,8,2]{2,0,1:T(2,128)(2,1)} copy(bf16[2,8,2]{2,1,0:T(8,128)(2,1)S(1)} %all_to_all.8) | data formatting | bytes 128 | tf_op jit(solution)/shard_map/all_to_all | solution.py:73
  1.5 5.2 %all-to-all-start.1 = ((bf16[2,8,2]{2,0,1:T(2,128)(2,1)}), bf16[2,8,2]{2,0,1:T(2,128)(2,1)S(1)}, u32[]{:S(2)}, u32[]{:S(2)}) async-start(bf16[2,8,2]{2,0,1:T(2,128)(2,1)} %copy.53), calls=%async_computation.1 | async-start | bytes 8192 | tf_op jit(solution)/shard_map/all_to_all | solution.py:73
  6.7 0.2 fusion.25
  6.9 1.1 %fusion.12 = f32[2,16,256]{2,1,0:T(8,128)S(1)} fusion(bf16[128,256]{1,0:T(8,128)(2,1)} %param.11, bf16[2,16,128]{2,1,0:T(8,128)(2,1)S(1)} %copy-done.1, f32[2,16]{1,0:T(2,128)S(1)} %add_sqrt_fusion.3, f32[2,16]{1,0:T(2,128)S(1)} %broadcast_multiply_fusion.3), kind=kOutput, calls=%fused_computation.18 | convolution fusion | flops 2113536 | bytes 106752 | tf_op jit(solution)/shard_map/dot_general | solution.py:16
  8.0 0.2 fusion.14
  8.3 9.7 %all_gather.6 = bf16[16,16,128]{2,1,0:T(8,128)(2,1)S(1)} all-gather(bf16[2,16,128]{2,1,0:T(8,128)(2,1)S(1)} %get-tuple-element.10), channel_id=1, replica_groups=mesh['dap'=8,'dp'=4] {'dap'}, dimensions={0}, use_global_device_ids=true | all-gather | bytes 73728 | tf_op jit(solution)/shard_map/all_gather | solution.py:79
  18.0 0.4 %copy.51 = bf16[16,16,128]{1,0,2:T(8,128)(2,1)S(1)} copy(bf16[16,16,128]{2,1,0:T(8,128)(2,1)S(1)} %all_gather.6) | data formatting | bytes 131072 | tf_op jit(solution)/shard_map/all_gather | solution.py:79
  18.4 0.1 copy.50
  18.6 0.4 fusion.60
  19.1 0.2 multiply_reduce_fusion.1
  19.3 0.6 %copy.48 = bf16[2,16,128]{2,0,1:T(2,128)(2,1)} copy(bf16[2,16,128]{2,1,0:T(8,128)(2,1)S(1)} %copy-done.1) | data formatting | bytes 16384 | tf_op args[0]
  19.9 3.3 %all-to-all-start = ((bf16[2,16,128]{2,0,1:T(2,128)(2,1)}), bf16[2,16,128]{2,0,1:T(2,128)(2,1)S(1)}, u32[]{:S(2)}, u32[]{:S(2)}) async-start(bf16[2,16,128]{2,0,1:T(2,128)(2,1)} %copy.48), calls=%async_computation | async-start | bytes 16384 | tf_op jit(solution)/shard_map/all_to_all | solution.py:72
  23.3 0.1 copy.63
  23.4 4.5 %all-to-all-done = bf16[2,16,128]{2,0,1:T(2,128)(2,1)S(1)} async-done(((bf16[2,16,128]{2,0,1:T(2,128)(2,1)}), bf16[2,16,128]{2,0,1:T(2,128)(2,1)S(1)}, u32[]{:S(2)}, u32[]{:S(2)}) %all-to-all-start) | async-done | bytes 8224 | tf_op jit(solution)/shard_map/all_to_all | solution.py:72
  28.0 0.2 fusion.42
  28.4 0.6 %copy-done.5 = bf16[128,128]{1,0:T(8,128)(2,1)S(1)} copy-done((bf16[128,128]{1,0:T(8,128)(2,1)S(1)}, bf16[128,128]{1,0:T(8,128)(2,1)}, u32[]{:S(2)}) %copy-start.5) | copy-done | bytes 32792
  29.0 0.2 fusion.8
  29.2 0.6 %copy-done.6 = bf16[128,128]{1,0:T(8,128)(2,1)S(1)} copy-done((bf16[128,128]{1,0:T(8,128)(2,1)S(1)}, bf16[128,128]{1,0:T(8,128)(2,1)}, u32[]{:S(2)}) %copy-start.6) | copy-done | bytes 32792
  29.7 0.3 fusion.57
  30.0 0.2 multiply_reduce_fusion
  30.3 0.1 fusion.58
  30.6 0.6 %copy-done.3 = bf16[128,4]{0,1:T(4,128)(2,1)S(1)} copy-done((bf16[128,4]{0,1:T(4,128)(2,1)S(1)}, bf16[128,4]{0,1:T(4,128)(2,1)}, u32[]{:S(2)}) %copy-start.3) | copy-done | bytes 1048
  31.2 0.1 fusion.9
  31.3 8.0 %all_gather.7 = bf16[4,16,16]{1,0,2:T(4,128)(2,1)S(1)} all-gather(bf16[4,16,2]{1,0,2:T(4,128)(2,1)S(1)} %fusion.9), channel_id=1, replica_groups=mesh['dap'=8,'dp'=4] {'dap'}, dimensions={2}, use_global_device_ids=true | all-gather | bytes 2304 | tf_op jit(solution)/shard_map/all_gather | solution.py:50
  39.3 0.1 copy.57
  39.4 0.1 fusion.4
  39.7 0.2 convolution_bitcast_fusion
  39.9 0.1 reshape.137
  40.0 0.7 %copy-done.2 = bf16[128,128]{1,0:T(8,128)(2,1)S(1)} copy-done((bf16[128,128]{1,0:T(8,128)(2,1)S(1)}, bf16[128,128]{1,0:T(8,128)(2,1)}, u32[]{:S(2)}) %copy-start.2) | copy-done | bytes 32792
  40.7 0.1 convolution_add_fusion
  40.8 0.6 %copy.61 = f32[16,2,128]{2,1,0:T(2,128)} copy(f32[16,2,128]{2,0,1:T(8,128)S(1)} %convolution_add_fusion) | data formatting | bytes 32768 | tf_op jit(solution)/shard_map/add | solution.py:62
  (39 shorter events, 1.2 us)
Async XLA Ops:
  0.0 30.3 %copy-start = (bf16[128,512]{1,0:T(8,128)(2,1)S(1)}, bf16[128,512]{1,0:T(8,128)(2,1)}, u32[]{:S(2)}) copy-start(bf16[128,512]{1,0:T(8,128)(2,1)} %param.15) | copy-start | bytes 393220
  0.8 5.8 %copy-start.1 = (bf16[2,16,128]{2,1,0:T(8,128)(2,1)S(1)}, bf16[2,16,128]{2,1,0:T(8,128)(2,1)}, u32[]{:S(2)}) copy-start(bf16[2,16,128]{2,1,0:T(8,128)(2,1)} %param.9) | copy-start | bytes 24580
  1.5 18.5 %all-to-all-start.1 = ((bf16[2,8,2]{2,0,1:T(2,128)(2,1)}), bf16[2,8,2]{2,0,1:T(2,128)(2,1)S(1)}, u32[]{:S(2)}, u32[]{:S(2)}) async-start(bf16[2,8,2]{2,0,1:T(2,128)(2,1)} %copy.53), calls=%async_computation.1 | async-start | bytes 8192 | tf_op jit(solution)/shard_map/all_to_all | solution.py:73
  6.9 1.1 %copy-start.4 = (bf16[128,256]{1,0:T(8,128)(2,1)S(1)}, bf16[128,256]{1,0:T(8,128)(2,1)}, u32[]{:S(2)}) copy-start(bf16[128,256]{1,0:T(8,128)(2,1)} %param.12) | copy-start | bytes 196612
  19.9 8.0 %all-to-all-start = ((bf16[2,16,128]{2,0,1:T(2,128)(2,1)}), bf16[2,16,128]{2,0,1:T(2,128)(2,1)S(1)}, u32[]{:S(2)}, u32[]{:S(2)}) async-start(bf16[2,16,128]{2,0,1:T(2,128)(2,1)} %copy.48), calls=%async_computation | async-start | bytes 16384 | tf_op jit(solution)/shard_map/all_to_all | solution.py:72
  28.2 0.8 %copy-start.5 = (bf16[128,128]{1,0:T(8,128)(2,1)S(1)}, bf16[128,128]{1,0:T(8,128)(2,1)}, u32[]{:S(2)}) copy-start(bf16[128,128]{1,0:T(8,128)(2,1)} %param.13) | copy-start | bytes 98308
  29.0 0.8 %copy-start.6 = (bf16[128,128]{1,0:T(8,128)(2,1)S(1)}, bf16[128,128]{1,0:T(8,128)(2,1)}, u32[]{:S(2)}) copy-start(bf16[128,128]{1,0:T(8,128)(2,1)} %param.14) | copy-start | bytes 98308
  30.5 0.7 %copy-start.3 = (bf16[128,4]{0,1:T(4,128)(2,1)S(1)}, bf16[128,4]{0,1:T(4,128)(2,1)}, u32[]{:S(2)}) copy-start(bf16[128,4]{0,1:T(4,128)(2,1)} %param.16) | copy-start | bytes 3076
  39.9 0.8 %copy-start.2 = (bf16[128,128]{1,0:T(8,128)(2,1)S(1)}, bf16[128,128]{1,0:T(8,128)(2,1)}, u32[]{:S(2)}) copy-start(bf16[128,128]{1,0:T(8,128)(2,1)} %param.17) | copy-start | bytes 98308
where the time goes:
time: 42 us; the launch traced here: 41.4 us
  blocking collectives  17.7 us (42%)
  starting transfers between devices  8.53 us (20%)
  local copies, waits for them, and re-layouts  5.7 us (14%)
  waiting for transfers between devices  4.51 us (11%)
  matrix products  2.83 us (7%)
  other arithmetic  1.97 us (5%)
    all_gather x1, blocking collectives, shards(): lax.all_gather(left_edge, 'dap', axis=0, tiled=True)  9.75 us
    all_gather x1, blocking collectives, attention(): bias = lax.all_gather(bias_part, 'dap', axis=2, tiled=True)  7.98 us
    all_to_all x1, starting transfers between devices, shards(): lax.all_to_all(pair_mask.astype(jnp.bfloat16), 'dap', split_axis=1, conca...  5.2 us
    all_to_all x1, waiting for transfers between devices, shards(): lax.all_to_all(pair, 'dap', split_axis=1, concat_axis=0, tiled=True)  4.51 us
    all_to_all x1, starting transfers between devices, shards(): lax.all_to_all(pair, 'dap', split_axis=1, concat_axis=0, tiled=True)  3.33 us
    unnamed x15, local copies, waits for them, and re-layouts  3 us
    dot_general x6, matrix products, matmul(): jnp.dot(flat, w, preferred_element_type=jnp.float32)  1.99 us
  transfers between devices with their start and end apart: 2, of which 1 were waited for; matrix products, arithmetic and copies ran while one was open for 9% of the time, Pallas kernels for 0%

commit v1 on v0

--- a/solution.py
+++ b/solution.py
@@ -70,8 +70,14 @@
     right_edge = edges(zn, w_right, maskf, hidden)
     pair_cols, mask_cols = (
         lax.all_to_all(pair, "dap", split_axis=1, concat_axis=0, tiled=True),
-        lax.all_to_all(
-            pair_mask.astype(jnp.bfloat16), "dap", split_axis=1, concat_axis=0, tiled=True
+        jnp.concatenate(
+            lax.all_to_all(
+                jnp.stack(jnp.split(pair_mask.astype(jnp.bfloat16), lax.axis_size("dap"), axis=1)),
+                "dap",
+                0,
+                0,
+            ),
+            axis=0,
         ),
     )
     tri = jnp.einsum(

time: 42 us -> 46.1 us (1.098)
  local copies, waits for them, and re-layouts: 5.7 us -> 10.1 us
    unnamed x15 -> x22, local copies, waits for them, and re-layouts: 3 us -> 7.27 us
    another operation x0 -> x1, local copies, waits for them, and re-layouts: none -> 0.59 us  [shards(): jnp.stack(jnp.split(pair_mask.astype(jnp.bfloat16), lax.axis_size('dap'),...]
    all_to_all x2 -> x1, local copies, waits for them, and re-layouts: 0.69 us -> 0.1 us  [shards(): lax.all_to_all(jnp.stack(jnp.split(pair_mask.astype(jnp.bfloat16), lax.ax...]
  transfers between devices with their start and end apart: 2 -> 2, of which waited for: 1 -> 1; matrix products, arithmetic and copies ran while one was open for 9% -> 8% of each run, Pallas kernels for 0% -> 0%
where the time goes in v1:
time: 46.1 us; the launch traced here: 45.6 us
  blocking collectives  17.7 us (38%)
  local copies, waits for them, and re-layouts  10.1 us (22%)
  starting transfers between devices  8.53 us (19%)
  waiting for transfers between devices  4.34 us (9%)
  matrix products  2.83 us (6%)
  other arithmetic  1.97 us (4%)
    all_gather x1, blocking collectives, shards(): lax.all_gather(left_edge, 'dap', axis=0, tiled=True)  9.75 us
    all_gather x1, blocking collectives, attention(): bias = lax.all_gather(bias_part, 'dap', axis=2, tiled=True)  7.98 us
    unnamed x22, local copies, waits for them, and re-layouts  7.27 us
    all_to_all x1, starting transfers between devices, shards(): lax.all_to_all(jnp.stack(jnp.split(pair_mask.astype(jnp.bfloat16), lax.ax...  5.2 us
    all_to_all x1, waiting for transfers between devices, shards(): lax.all_to_all(pair, 'dap', split_axis=1, concat_axis=0, tiled=True)  4.34 us
    all_to_all x1, starting transfers between devices, shards(): lax.all_to_all(pair, 'dap', split_axis=1, concat_axis=0, tiled=True)  3.33 us
    dot_general x6, matrix products, matmul(): jnp.dot(flat, w, preferred_element_type=jnp.float32)  1.99 us
  transfers between devices with their start and end apart: 2, of which 1 were waited for; matrix products, arithmetic and copies ran while one was open for 8% of the time, Pallas kernels for 0%

profile of v1, /device:TPU:0, one launch (start us, length us, event | category | flops | bytes accessed | tf_op | source)
XLA Modules:
  0.0 45.6 jit_solution(15004590528022742447)
XLA Ops:
  0.0 0.8 %fusion.56 = (bf16[2,16]{1,0:T(2,128)(2,1)S(1)}, f32[2,16]{1,0:T(2,128)S(1)}) fusion(s32[2,16]{1,0:T(2,128)} %param.10), kind=kLoop, calls=%fused_computation.93 | loop fusion | flops 64 | bytes 320 | tf_op jit(solution)/shard_map/convert_element_type | solution.py:75
  0.8 0.6 %constant_dynamic-update-slice_fusion.7 = bf16[8,2,2]{2,1,0:T(2,128)(2,1)} fusion(bf16[2,16]{1,0:T(2,128)(2,1)S(1)} %get-tuple-element.8), kind=kLoop, calls=%fused_computation.41 | loop fusion | bytes 520
  1.4 0.6 %constant_dynamic-update-slice_fusion.6 = bf16[8,2,2]{2,1,0:T(2,128)(2,1)} fusion(bf16[8,2,2]{2,1,0:T(2,128)(2,1)} %constant_dynamic-update-slice_fusion.7, bf16[2,16]{1,0:T(2,128)(2,1)S(1)} %get-tuple-element.8), kind=kLoop, calls=%fused_computation.40 | loop fusion | bytes 520
  1.9 0.6 %constant_dynamic-update-slice_fusion.5 = bf16[8,2,2]{2,1,0:T(2,128)(2,1)} fusion(bf16[8,2,2]{2,1,0:T(2,128)(2,1)} %constant_dynamic-update-slice_fusion.6, bf16[2,16]{1,0:T(2,128)(2,1)S(1)} %get-tuple-element.8), kind=kLoop, calls=%fused_computation.39 | loop fusion | bytes 520
  2.5 0.7 %constant_dynamic-update-slice_fusion.4 = bf16[8,2,2]{2,1,0:T(2,128)(2,1)} fusion(bf16[8,2,2]{2,1,0:T(2,128)(2,1)} %constant_dynamic-update-slice_fusion.5, bf16[2,16]{1,0:T(2,128)(2,1)S(1)} %get-tuple-element.8), kind=kLoop, calls=%fused_computation.38 | loop fusion | bytes 520
  3.2 0.6 %constant_dynamic-update-slice_fusion.3 = bf16[8,2,2]{2,1,0:T(2,128)(2,1)} fusion(bf16[8,2,2]{2,1,0:T(2,128)(2,1)} %constant_dynamic-update-slice_fusion.4, bf16[2,16]{1,0:T(2,128)(2,1)S(1)} %get-tuple-element.8), kind=kLoop, calls=%fused_computation.37 | loop fusion | bytes 520
  3.8 0.6 %constant_dynamic-update-slice_fusion.2 = bf16[8,2,2]{2,1,0:T(2,128)(2,1)} fusion(bf16[8,2,2]{2,1,0:T(2,128)(2,1)} %constant_dynamic-update-slice_fusion.3, bf16[2,16]{1,0:T(2,128)(2,1)S(1)} %get-tuple-element.8), kind=kLoop, calls=%fused_computation.36 | loop fusion | bytes 520
  4.4 0.6 %constant_dynamic-update-slice_fusion.1 = bf16[8,2,2]{2,1,0:T(2,128)(2,1)} fusion(bf16[8,2,2]{2,1,0:T(2,128)(2,1)} %constant_dynamic-update-slice_fusion.2, bf16[2,16]{1,0:T(2,128)(2,1)S(1)} %get-tuple-element.8), kind=kLoop, calls=%fused_computation.35 | loop fusion | bytes 520
  5.0 0.6 %constant_dynamic-update-slice_fusion = bf16[8,2,2]{2,1,0:T(2,128)(2,1)} fusion(bf16[8,2,2]{2,1,0:T(2,128)(2,1)} %constant_dynamic-update-slice_fusion.1, bf16[2,16]{1,0:T(2,128)(2,1)S(1)} %get-tuple-element.8), kind=kLoop, calls=%fused_computation.34 | loop fusion | bytes 520 | tf_op jit(solution)/shard_map/stack | solution.py:75
  5.6 5.2 %all-to-all-start.1 = ((bf16[8,2,2]{2,1,0:T(2,128)(2,1)}), bf16[8,2,2]{2,1,0:T(2,128)(2,1)S(1)}, u32[]{:S(2)}, u32[]{:S(2)}) async-start(bf16[8,2,2]{2,1,0:T(2,128)(2,1)} %constant_dynamic-update-slice_fusion), calls=%async_computation.1 | async-start | bytes 8192 | tf_op jit(solution)/shard_map/all_to_all | solution.py:74
  10.9 0.2 fusion.25
  11.1 1.1 %fusion.12 = f32[2,16,256]{2,1,0:T(8,128)S(1)} fusion(bf16[128,256]{1,0:T(8,128)(2,1)} %param.11, bf16[2,16,128]{2,1,0:T(8,128)(2,1)S(1)} %copy-done.1, f32[2,16]{1,0:T(2,128)S(1)} %add_sqrt_fusion.3, f32[2,16]{1,0:T(2,128)S(1)} %broadcast_multiply_fusion.3), kind=kOutput, calls=%fused_computation.18 | convolution fusion | flops 2113536 | bytes 106752 | tf_op jit(solution)/shard_map/dot_general | solution.py:16
  12.2 0.2 fusion.14
  12.5 9.7 %all_gather.6 = bf16[16,16,128]{2,1,0:T(8,128)(2,1)S(1)} all-gather(bf16[2,16,128]{2,1,0:T(8,128)(2,1)S(1)} %get-tuple-element.10), channel_id=1, replica_groups=mesh['dap'=8,'dp'=4] {'dap'}, dimensions={0}, use_global_device_ids=true | all-gather | bytes 73728 | tf_op jit(solution)/shard_map/all_gather | solution.py:85
  22.2 0.4 copy.93
  22.8 0.4 fusion.60
  23.3 0.2 multiply_reduce_fusion.1
  23.5 0.6 %copy.90 = bf16[2,16,128]{2,0,1:T(2,128)(2,1)} copy(bf16[2,16,128]{2,1,0:T(8,128)(2,1)S(1)} %copy-done.1) | data formatting | bytes 16384 | tf_op args[0]
  24.1 3.3 %all-to-all-start = ((bf16[2,16,128]{2,0,1:T(2,128)(2,1)}), bf16[2,16,128]{2,0,1:T(2,128)(2,1)S(1)}, u32[]{:S(2)}, u32[]{:S(2)}) async-start(bf16[2,16,128]{2,0,1:T(2,128)(2,1)} %copy.90), calls=%async_computation | async-start | bytes 16384 | tf_op jit(solution)/shard_map/all_to_all | solution.py:72
  27.8 4.3 %all-to-all-done = bf16[2,16,128]{2,0,1:T(2,128)(2,1)S(1)} async-done(((bf16[2,16,128]{2,0,1:T(2,128)(2,1)}), bf16[2,16,128]{2,0,1:T(2,128)(2,1)S(1)}, u32[]{:S(2)}, u32[]{:S(2)}) %all-to-all-start) | async-done | bytes 8224 | tf_op jit(solution)/shard_map/all_to_all | solution.py:72
  32.2 0.2 fusion.42
  32.6 0.6 %copy-done.5 = bf16[128,128]{1,0:T(8,128)(2,1)S(1)} copy-done((bf16[128,128]{1,0:T(8,128)(2,1)S(1)}, bf16[128,128]{1,0:T(8,128)(2,1)}, u32[]{:S(2)}) %copy-start.5) | copy-done | bytes 32792
  33.1 0.2 fusion.8
  33.3 0.6 %copy-done.6 = bf16[128,128]{1,0:T(8,128)(2,1)S(1)} copy-done((bf16[128,128]{1,0:T(8,128)(2,1)S(1)}, bf16[128,128]{1,0:T(8,128)(2,1)}, u32[]{:S(2)}) %copy-start.6) | copy-done | bytes 32792
  33.9 0.3 fusion.57
  34.2 0.2 multiply_reduce_fusion
  34.8 0.6 %copy-done.3 = bf16[128,4]{0,1:T(4,128)(2,1)S(1)} copy-done((bf16[128,4]{0,1:T(4,128)(2,1)S(1)}, bf16[128,4]{0,1:T(4,128)(2,1)}, u32[]{:S(2)}) %copy-start.3) | copy-done | bytes 1048
  35.5 8.0 %all_gather.7 = bf16[4,16,16]{1,0,2:T(4,128)(2,1)S(1)} all-gather(bf16[4,16,2]{1,0,2:T(4,128)(2,1)S(1)} %fusion.9), channel_id=1, replica_groups=mesh['dap'=8,'dp'=4] {'dap'}, dimensions={2}, use_global_device_ids=true | all-gather | bytes 2304 | tf_op jit(solution)/shard_map/all_gather | solution.py:50
  43.6 0.1 fusion.4
  43.9 0.2 convolution_bitcast_fusion
  44.2 0.7 %copy-done.2 = bf16[128,128]{1,0:T(8,128)(2,1)S(1)} copy-done((bf16[128,128]{1,0:T(8,128)(2,1)S(1)}, bf16[128,128]{1,0:T(8,128)(2,1)}, u32[]{:S(2)}) %copy-start.2) | copy-done | bytes 32792
  45.0 0.6 %copy.103 = f32[16,2,128]{2,1,0:T(2,128)} copy(f32[16,2,128]{2,0,1:T(8,128)S(1)} %convolution_add_fusion) | data formatting | bytes 32768 | tf_op jit(solution)/shard_map/add | solution.py:62
  (46 shorter events, 2.1 us)
Async XLA Ops:
  0.0 34.5 %copy-start = (bf16[128,512]{1,0:T(8,128)(2,1)S(1)}, bf16[128,512]{1,0:T(8,128)(2,1)}, u32[]{:S(2)}) copy-start(bf16[128,512]{1,0:T(8,128)(2,1)} %param.15) | copy-start | bytes 393220
  3.2 7.7 %copy-start.1 = (bf16[2,16,128]{2,1,0:T(8,128)(2,1)S(1)}, bf16[2,16,128]{2,1,0:T(8,128)(2,1)}, u32[]{:S(2)}) copy-start(bf16[2,16,128]{2,1,0:T(8,128)(2,1)} %param.9) | copy-start | bytes 24580
  5.6 18.5 %all-to-all-start.1 = ((bf16[8,2,2]{2,1,0:T(2,128)(2,1)}), bf16[8,2,2]{2,1,0:T(2,128)(2,1)S(1)}, u32[]{:S(2)}, u32[]{:S(2)}) async-start(bf16[8,2,2]{2,1,0:T(2,128)(2,1)} %constant_dynamic-update-slice_fusion), calls=%async_computation.1 | async-start | bytes 8192 | tf_op jit(solution)/shard_map/all_to_all | solution.py:74
  11.1 1.1 %copy-start.4 = (bf16[128,256]{1,0:T(8,128)(2,1)S(1)}, bf16[128,256]{1,0:T(8,128)(2,1)}, u32[]{:S(2)}) copy-start(bf16[128,256]{1,0:T(8,128)(2,1)} %param.12) | copy-start | bytes 196612
  24.1 8.0 %all-to-all-start = ((bf16[2,16,128]{2,0,1:T(2,128)(2,1)}), bf16[2,16,128]{2,0,1:T(2,128)(2,1)S(1)}, u32[]{:S(2)}, u32[]{:S(2)}) async-start(bf16[2,16,128]{2,0,1:T(2,128)(2,1)} %copy.90), calls=%async_computation | async-start | bytes 16384 | tf_op jit(solution)/shard_map/all_to_all | solution.py:72
  32.4 0.8 %copy-start.5 = (bf16[128,128]{1,0:T(8,128)(2,1)S(1)}, bf16[128,128]{1,0:T(8,128)(2,1)}, u32[]{:S(2)}) copy-start(bf16[128,128]{1,0:T(8,128)(2,1)} %param.13) | copy-start | bytes 98308
  33.1 0.8 %copy-start.6 = (bf16[128,128]{1,0:T(8,128)(2,1)S(1)}, bf16[128,128]{1,0:T(8,128)(2,1)}, u32[]{:S(2)}) copy-start(bf16[128,128]{1,0:T(8,128)(2,1)} %param.14) | copy-start | bytes 98308
  34.7 0.7 %copy-start.3 = (bf16[128,4]{0,1:T(4,128)(2,1)S(1)}, bf16[128,4]{0,1:T(4,128)(2,1)}, u32[]{:S(2)}) copy-start(bf16[128,4]{0,1:T(4,128)(2,1)} %param.16) | copy-start | bytes 3076
  44.1 0.8 %copy-start.2 = (bf16[128,128]{1,0:T(8,128)(2,1)S(1)}, bf16[128,128]{1,0:T(8,128)(2,1)}, u32[]{:S(2)}) copy-start(bf16[128,128]{1,0:T(8,128)(2,1)} %param.17) | copy-start | bytes 98308
